TPU v7x, 256 devices: a whole 4x4x8 slice. The times are simulated.
256 devices in a mesh: rows: 16 (over z, core), strata: 16 (over y, x).
Axes of the slice: x: 4, y: 4, z: 8, core: 2. Of those that a mesh axis runs over, the one named last changes fastest.
Arguments:
- user_factors: float32 [32768, 512], P(('rows', 'strata')), may hold values from -1.3 to 1.3
- item_factors: float32 [131072, 512], P(('rows', 'strata')), may hold values from -1.3 to 1.3
- ratings: float32 [2, 262144], P(None, ('rows', 'strata')), may hold values from -6 to 6
- user_offsets: int32 [2, 262144], P(None, ('rows', 'strata')), may hold values from 0 to 2047, as said below
- item_offsets: int32 [2, 262144], P(None, ('rows', 'strata')), may hold values from 0 to 511
- counts: int32 [2, 256], P(None, ('rows', 'strata')), may hold values from 128 to 1024, as said below
Outputs:
- new_users: float32 [32768, 512], P(('rows', 'strata'))
- new_items: float32 [131072, 512], P(('rows', 'strata'))
Inputs may be any that keep to these rules, and one draw needn't show every extreme that they name: `counts`: some tile of each sub-epoch has all 1024 slots active. `user_offsets`: splitting a user block into 16 runs of 128 users, each tile's slots (active or not) name exactly 32 distinct users of every run.
All inputs are finite; a program needn't handle non-finite values.
Results may differ from a plain program's by a relative error of at most 0.0003.
Values sent between devices are 32-bit elements; how exact they have to be, the bound alone decides.
A program may use at most 64 MiB of HBM per device.

v0:
```python
import jax
import jax.numpy as jnp
from jax import lax
from jax.sharding import PartitionSpec as P


def passed_along(value, axis, steps):
    count = lax.axis_size(axis)
    pairs = [(source, (source + steps) % count) for source in range(count)]
    return lax.ppermute(value, axis, pairs)


def tile_grads(block_u, block_v, user_index, item_index, observed, count):
    slots = jnp.arange(observed.shape[0], dtype=jnp.int32)
    active_mask = (slots < count).astype(jnp.float32)
    u_rows = block_u[user_index]
    v_rows = block_v[item_index]
    errors = active_mask * (observed - jnp.sum(u_rows * v_rows, axis=1))
    grad_u = jnp.zeros_like(block_u).at[user_index].add(errors[:, None] * v_rows)
    grad_v = jnp.zeros_like(block_v).at[item_index].add(errors[:, None] * u_rows)
    return (grad_u, grad_v)


def gather_users(owned_rows):
    return lax.all_gather(owned_rows, "strata", axis=0, tiled=True)


def on_device(user_factors, item_factors, ratings, user_offsets, item_offsets, counts):
    owned_rows = user_factors
    block_v = item_factors
    block_u = gather_users(owned_rows)
    sub_epochs = ratings.shape[0]
    for sub_epoch in range(sub_epochs):
        step_size = 0.04 / (1.0 + 0.5 * sub_epoch)
        grad_u, grad_v = tile_grads(
            block_u,
            block_v,
            user_offsets[sub_epoch],
            item_offsets[sub_epoch],
            ratings[sub_epoch],
            counts[sub_epoch, 0],
        )
        owned_share = lax.psum_scatter(grad_u, "strata", scatter_dimension=0, tiled=True)
        owned_rows = owned_rows + step_size * (owned_share - 0.1 * owned_rows)
        if sub_epoch + 1 < sub_epochs:
            block_u = gather_users(owned_rows)
        block_v = block_v + step_size * (grad_v - 0.1 * block_v)
        if sub_epoch + 1 < sub_epochs:
            block_v = passed_along(block_v, "rows", 1)
    block_v = passed_along(block_v, "rows", 1 - sub_epochs)
    return (owned_rows, block_v)


def solution(mesh):
    return jax.shard_map(
        on_device,
        mesh=mesh,
        in_specs=(
            P(("rows", "strata"), None),
            P(("rows", "strata"), None),
            P(None, ("rows", "strata")),
            P(None, ("rows", "strata")),
            P(None, ("rows", "strata")),
            P(None, ("rows", "strata")),
        ),
        out_specs=(P(("rows", "strata"), None), P(("rows", "strata"), None)),
        check_vma=False,
    )
```

profile of v0, /device:TPU:96, one launch (start us, length us, event | category | flops | bytes accessed | tf_op | source)
XLA Modules:
  0.0 340.7 jit_solution(11636655142841879035)
XLA Ops:
  7.2 0.7 all-gather.3.cloned.1.call-update
  7.9 0.8 compare_select_fusion
  8.8 6.5 %gather_fusion.1 = f32[1024,512]{1,0:T(8,128)} fusion(f32[512,512]{1,0:T(8,128)} %param.7, s32[1024]{0:T(1024)S(1)} %broadcast_clamp_fusion.1), kind=kCustom, calls=%fused_computation.1 | custom fusion | bytes 4198400 | tf_op jit(solution)/shard_map/gather | solution.py:17
  16.0 52.7 %all-gather.3.cloned.1.call-done = f32[2048,512]{1,0:T(8,128)} async-done(((f32[128,512]{1,0:T(8,128)}), f32[2048,512]{1,0:T(8,128)}) %all-gather.3.cloned.1.call-update) | async-done | bytes 4194320 | tf_op jit(solution)/shard_map/all_gather | solution.py:25
  68.7 6.2 %gather_fusion = f32[1024,512]{1,0:T(8,128)S(1)} fusion(f32[2048,512]{1,0:T(8,128)} %all-gather.3.cloned.1.call-done, s32[1024]{0:T(1024)S(1)} %broadcast_clamp_fusion.3), kind=kCustom, calls=%fused_computation | custom fusion | bytes 4198400 | tf_op jit(solution)/shard_map/gather | solution.py:16
  75.0 1.9 multiply_reduce_fusion.1
  76.8 0.7 subtract_select_fusion.1
  77.5 9.9 %scatter_custom_fusion = f32[2048,512]{1,0:T(8,128)} fusion(s32[1024]{0:T(1024)S(1)} %bitcast.25, f32[1024,512]{1,0:T(8,128)} %gather_fusion.1, f32[]{:T(128)} %constant.7.clone.1, f32[1024]{0:T(1024)S(1)} %subtract_select_fusion.1), kind=kCustom, calls=%fused_computation.15 | custom fusion | flops 1048576 | bytes 6295556 | tf_op jit(solution)/shard_map/scatter-add | solution.py:19
  87.5 83.3 %reduce-scatter.3.cloned.1.call-done = f32[128,512]{1,0:T(8,128)} async-done(((f32[2048,512]{1,0:T(8,128)}), f32[128,512]{1,0:T(8,128)}) %reduce-scatter.3.cloned.1.call-update) | async-done | bytes 262160 | tf_op jit(solution)/shard_map/reduce_scatter | solution.py:43
  170.8 1.7 multiply_add_fusion.3
  172.6 8.1 %scatter_custom_fusion.1 = f32[512,512]{1,0:T(8,128)} fusion(s32[1024]{0:T(1024)S(1)} %bitcast.23, f32[1024,512]{1,0:T(8,128)S(1)} %gather_fusion, f32[1024]{0:T(1024)S(1)} %subtract_select_fusion.1, f32[]{:T(128)} %constant.7.clone.1), kind=kCustom, calls=%fused_computation.13 | custom fusion | flops 1048576 | bytes 3149828 | tf_op jit(solution)/shard_map/scatter-add | solution.py:20
  180.7 1.5 multiply_add_fusion.1
  182.2 14.2 %collective-permute-done = f32[512,512]{1,0:T(8,128)S(1)} collective-permute-done((f32[512,512]{1,0:T(8,128)S(1)}, f32[512,512]{1,0:T(8,128)S(1)}, u32[]{:S(2)}, u32[]{:S(2)}) %collective-permute-start) | collective-permute-done | bytes 1048608 | tf_op jit(solution)/shard_map/ppermute | solution.py:10
  196.4 4.9 %gather_fusion.3 = f32[1024,512]{1,0:T(8,128)} fusion(f32[512,512]{1,0:T(8,128)S(1)} %collective-permute-done, s32[1024]{0:T(1024)S(1)} %broadcast_clamp_fusion), kind=kCustom, calls=%fused_computation.3 | custom fusion | bytes 4198400 | tf_op jit(solution)/shard_map/gather | solution.py:17
  201.3 28.2 %all-gather.5.cloned.1.call-done = f32[2048,512]{1,0:T(8,128)} async-done(((f32[128,512]{1,0:T(8,128)}), f32[2048,512]{1,0:T(8,128)}) %all-gather.5.cloned.1.call-update) | async-done | bytes 4194320 | tf_op jit(solution)/shard_map/all_gather | solution.py:25
  229.5 6.2 %gather_fusion.2 = f32[1024,512]{1,0:T(8,128)S(1)} fusion(f32[2048,512]{1,0:T(8,128)} %all-gather.5.cloned.1.call-done, s32[1024]{0:T(1024)S(1)} %broadcast_clamp_fusion.2), kind=kCustom, calls=%fused_computation.2 | custom fusion | bytes 4198400 | tf_op jit(solution)/shard_map/gather | solution.py:16
  235.7 1.9 multiply_reduce_fusion
  238.2 9.9 %scatter_custom_fusion.2 = f32[2048,512]{1,0:T(8,128)} fusion(s32[1024]{0:T(1024)S(1)} %bitcast.21, f32[1024,512]{1,0:T(8,128)} %gather_fusion.3, f32[]{:T(128)} %constant.7.clone.1, f32[1024]{0:T(1024)S(1)} %subtract_select_fusion), kind=kCustom, calls=%fused_computation.10 | custom fusion | flops 1048576 | bytes 6295556 | tf_op jit(solution)/shard_map/scatter-add | solution.py:19
  248.2 8.1 %scatter_custom_fusion.3 = f32[512,512]{1,0:T(8,128)} fusion(s32[1024]{0:T(1024)S(1)} %bitcast.19, f32[1024,512]{1,0:T(8,128)S(1)} %gather_fusion.2, f32[1024]{0:T(1024)S(1)} %subtract_select_fusion, f32[]{:T(128)} %constant.7.clone.1), kind=kCustom, calls=%fused_computation.8 | custom fusion | flops 1048576 | bytes 3149828 | tf_op jit(solution)/shard_map/scatter-add | solution.py:20
  256.3 1.5 multiply_add_fusion
  257.8 12.3 %collective-permute-done.1 = f32[512,512]{1,0:T(8,128)S(1)} collective-permute-done((f32[512,512]{1,0:T(8,128)S(1)}, f32[512,512]{1,0:T(8,128)S(1)}, u32[]{:S(2)}, u32[]{:S(2)}) %collective-permute-start.1) | collective-permute-done | bytes 1048608 | tf_op jit(solution)/shard_map/ppermute | solution.py:10
  270.1 61.4 %reduce-scatter.5.cloned.1.call-done = f32[128,512]{1,0:T(8,128)} async-done(((f32[2048,512]{1,0:T(8,128)}), f32[128,512]{1,0:T(8,128)}) %reduce-scatter.5.cloned.1.call-update) | async-done | bytes 262160 | tf_op jit(solution)/shard_map/reduce_scatter | solution.py:43
  331.5 1.7 multiply_add_fusion.2
  333.2 1.0 copy.9
  (29 shorter events, 1.6 us)
Async XLA Ops:
  7.2 61.6 %all-gather.3.cloned.1.call-start = ((), (), s32[]{:S(2)}) async-start(), calls=%async_computation.2 | async-start | bytes 4456448 | tf_op jit(solution)/shard_map/all_gather | solution.py:25
  7.9 162.9 %reduce-scatter.3.cloned.1.call-start = ((), (), s32[]{:S(2)}) async-start(), calls=%async_computation.3 | async-start | bytes 4456448 | tf_op jit(solution)/shard_map/reduce_scatter | solution.py:43
  8.7 6.6 %copy-start.5 = (s32[2,1]{0,1:T(1,128)S(1)}, s32[2,1]{0,1:T(1,128)}, u32[]{:S(2)}) copy-start(s32[2,1]{0,1:T(1,128)} %param.11) | copy-start | bytes 28
  8.8 7.2 %copy-start.3 = (s32[2,1024]{1,0:T(2,128)S(1)}, s32[2,1024]{1,0:T(2,128)}, u32[]{:S(2)}) copy-start(s32[2,1024]{1,0:T(2,128)} %param.9) | copy-start | bytes 24580
  8.8 7.2 %copy-start.4 = (f32[2,1024]{1,0:T(2,128)S(1)}, f32[2,1024]{1,0:T(2,128)}, u32[]{:S(2)}) copy-start(f32[2,1024]{1,0:T(2,128)} %param.8) | copy-start | bytes 24580
  87.4 83.4 %copy-start.2 = (f32[128,512]{1,0:T(8,128)S(1)}, f32[128,512]{1,0:T(8,128)}, u32[]{:S(2)}) copy-start(f32[128,512]{1,0:T(8,128)} %param.6) | copy-start | bytes 786436
  87.4 93.3 %copy-start = (f32[512,512]{1,0:T(8,128)S(1)}, f32[512,512]{1,0:T(8,128)}, u32[]{:S(2)}) copy-start(f32[512,512]{1,0:T(8,128)} %param.7) | copy-start | bytes 3145732
  87.5 142.0 %all-gather.5.cloned.1.call-start = ((), (), s32[]{:S(2)}) async-start(), calls=%async_computation.4 | async-start | bytes 4456448 | tf_op jit(solution)/shard_map/all_gather | solution.py:25
  172.5 159.0 %reduce-scatter.5.cloned.1.call-start = ((), (), s32[]{:S(2)}) async-start(), calls=%async_computation.5 | async-start | bytes 4456448 | tf_op jit(solution)/shard_map/reduce_scatter | solution.py:43
  182.2 14.2 %collective-permute-start = (f32[512,512]{1,0:T(8,128)S(1)}, f32[512,512]{1,0:T(8,128)S(1)}, u32[]{:S(2)}, u32[]{:S(2)}) collective-permute-start(f32[512,512]{1,0:T(8,128)S(1)} %multiply_add_fusion.1), channel_id=1, source_target_pairs={{0,16},{16,32},{32,48},{48,64},{64,80},{80,96},{96,112},{112,128},... | collective-permute-start | bytes 3145736 | tf_op jit(solution)/shard_map/ppermute | solution.py:10
  256.3 75.2 %copy-start.1 = (f32[128,512]{1,0:T(8,128)S(1)}, f32[128,512]{1,0:T(8,128)}, u32[]{:S(2)}) copy-start(f32[128,512]{1,0:T(8,128)} %multiply_add_fusion.3) | copy-start | bytes 786436
  257.8 12.3 %collective-permute-start.1 = (f32[512,512]{1,0:T(8,128)S(1)}, f32[512,512]{1,0:T(8,128)S(1)}, u32[]{:S(2)}, u32[]{:S(2)}) collective-permute-start(f32[512,512]{1,0:T(8,128)S(1)} %multiply_add_fusion), channel_id=1, source_target_pairs={{0,240},{16,0},{32,16},{48,32},{64,48},{80,64},{96,80},{112,96},{1... | collective-permute-start | bytes 3145736 | tf_op jit(solution)/shard_map/ppermute | solution.py:10
Sparse Core Ops, SparseCore 0:
  10.4 58.2 all-gather.2
  87.6 83.1 reduce-scatter.2
  173.8 55.6 all-gather.4
  248.3 83.1 reduce-scatter.4
where the time goes:
time: 342 us; the launch traced here: 341 us
  waiting for transfers between devices  253 us (74%)
  other arithmetic  48.3 us (14%)
  local copies, waits for them, and re-layouts  25.5 us (7%)
  between operations  13.9 us (4%)
    reduce_scatter x2, waiting for transfers between devices, on_device(): lax.psum_scatter(grad_u, 'strata', scatter_dimension=0, tiled=True)  145 us
    all_gather x2, waiting for transfers between devices, gather_users(): return lax.all_gather(owned_rows, 'strata', axis=0, tiled=True)  80.9 us
    ppermute x2, waiting for transfers between devices, passed_along(): return lax.ppermute(value, axis, pairs)  26.5 us
    scatter-add x2, other arithmetic, tile_grads(): jnp.zeros_like(block_u).at[user_index].add(errors[:, None] * v_rows)  19.9 us
    scatter-add x2, other arithmetic, tile_grads(): jnp.zeros_like(block_v).at[item_index].add(errors[:, None] * u_rows)  16.2 us
    gather x2, local copies, waits for them, and re-layouts, tile_grads(): u_rows = block_u[user_index]  12.4 us
    gather x2, local copies, waits for them, and re-layouts, tile_grads(): v_rows = block_v[item_index]  11.4 us
  transfers between devices with their start and end apart: 6, of which 6 were waited for; matrix products, arithmetic and copies ran while one was open for 9% of the time, Pallas kernels for 0%

commit v1 on v0

v1 whole, which is shorter than its diff:
```python
import functools

import jax
import jax.numpy as jnp
from jax import lax
from jax.experimental import pallas as pl
from jax.experimental.pallas import tpu as pltpu
from jax.sharding import PartitionSpec as P

MESH = pl.DeviceIdType.MESH
F32 = jnp.float32
BF16 = jnp.bfloat16

SIDE = 4
OWNERS = SIDE * SIDE
RUN = 128
TOUCH = 32
GROUPS = SIDE
ORDER = (0, 1, 3, 2)

NN = (((1,), (0,)), ((), ()))
NT = (((1,), (1,)), ((), ()))
TN = (((0,), (0,)), ((), ()))


def mm(a, b, dims):
    return lax.dot_general(a, b, dims, preferred_element_type=F32)


def halves(value):
    top = value.astype(BF16)
    return top, (value - top.astype(F32)).astype(BF16)


def mm3(a, b, dims):
    return mm(a[0], b[0], dims) + mm(a[0], b[1], dims) + mm(a[1], b[0], dims)


def iota(shape, dim):
    return lax.broadcasted_iota(jnp.int32, shape, dim)


def onehot(test):
    return jnp.where(test, 1.0, 0.0).astype(BF16)


def steps_of(sub_epoch):
    return 0.04 / (1.0 + 0.5 * sub_epoch)


def kernel(
    n_rows,
    u_hbm, v_hbm, rate_ref, user_ref, item_ref, count_ref,
    out_u, out_v,
    u_own, v_cur, v_new, v_hi, v_lo,
    mask_send, mask_recv, rank_tab, pos_tab,
    sel, sel_t,
    b_one, b_hi, b_lo, num, rat,
    ut_hi, ut_lo, w_hi, w_lo,
    u_send, u_recv, g_send, g_recv, u_parts,
    load_sem, mask_ss, mask_rs, u_ss, u_rs, g_ss, g_rs, v_ss, v_rs,
):
    row = lax.axis_index("rows")
    place = lax.axis_index("strata")
    y, x = place // SIDE, place % SIDE
    up, down = (row + 1) % n_rows, (row + n_rows - 1) % n_rows
    items = v_cur.shape[0]
    entries = rate_ref.shape[1]
    subs = rate_ref.shape[0]

    def away(slot, sign):
        dy, dx = slot // SIDE, slot % SIDE
        return ((y + sign * dy + SIDE) % SIDE) * SIDE + (x + sign * dx + SIDE) % SIDE

    def tile_of(slot):
        return (row, away(slot, 1))

    def owner_of(slot):
        return (row, away(slot, -1))

    barrier = pltpu.get_barrier_semaphore()
    for slot in range(1, OWNERS):
        pl.semaphore_signal(barrier, inc=1, device_id=tile_of(slot), device_id_type=MESH)
    for other in (up, down):
        pl.semaphore_signal(barrier, inc=1, device_id=(other, place), device_id_type=MESH)

    load_u = pltpu.make_async_copy(u_hbm, u_own, load_sem.at[0])
    load_v = pltpu.make_async_copy(v_hbm, v_cur, load_sem.at[1])
    load_u.start()
    load_v.start()

    def slot_and_run(t):
        user = user_ref[t : t + 1, :]
        owner = user >> 7
        dy = (y + SIDE - (owner >> 2)) & 3
        dx = (x + SIDE - (owner & 3)) & 3
        return dy * SIDE + dx, user & (RUN - 1)

    for t in range(subs):
        slot_e, low_e = slot_and_run(t)
        hot_slot = onehot(iota((OWNERS, entries), 0) == slot_e)
        hot_low = onehot(iota((RUN, entries), 0) == low_e)
        named = jnp.where(mm(hot_slot, hot_low, NT) > 0.5, 1.0, 0.0)
        mask_send[:, t, :] = named
        before = onehot(iota((RUN, RUN), 0) < iota((RUN, RUN), 1))
        rank = mm(named.astype(BF16), before, NN)
        each = mm(rank.astype(BF16), hot_low, NN)
        rank_e = jnp.sum(jnp.where(iota((OWNERS, entries), 0) == slot_e, each, 0.0), axis=0, keepdims=True)
        pos_tab[t : t + 1, :] = slot_e.astype(F32) * float(TOUCH) + rank_e

    pl.semaphore_wait(barrier, OWNERS + 1)

    def mask_copy(slot):
        return pltpu.make_async_remote_copy(
            src_ref=mask_send.at[slot], dst_ref=mask_recv.at[slot],
            send_sem=mask_ss.at[slot], recv_sem=mask_rs.at[slot],
            device_id=owner_of(slot), device_id_type=MESH)

    def u_copy(t, slot):
        return pltpu.make_async_remote_copy(
            src_ref=u_send.at[t, slot], dst_ref=u_recv.at[t, slot],
            send_sem=u_ss.at[t, slot], recv_sem=u_rs.at[t, slot],
            device_id=tile_of(slot), device_id_type=MESH)

    def g_copy(t, slot):
        return pltpu.make_async_remote_copy(
            src_ref=g_send.at[t, slot], dst_ref=g_recv.at[t, slot],
            send_sem=g_ss.at[t, slot], recv_sem=g_rs.at[t, slot],
            device_id=owner_of(slot), device_id_type=MESH)

    def slots_of(group):
        return range(group * SIDE, (group + 1) * SIDE)

    def rows_of(group):
        return slice(group * RUN, (group + 1) * RUN)

    for group in ORDER:
        for slot in slots_of(group):
            if slot:
                mask_copy(slot).start()
    mask_recv[0] = mask_send[0]

    load_u.wait()
    top, low = halves(u_own[...])
    u_parts[0] = top
    u_parts[1] = low

    def one_hot_items(t):
        active = iota((1, entries), 1) < count_ref[t : t + 1, 0:1]
        rate = rate_ref[t : t + 1, :]
        rate_top = rate.astype(BF16).astype(F32)
        rate_low = rate - rate_top
        item = jnp.where(active, item_ref[t : t + 1, :], -1)
        step = 64

        def body(i, _):
            at = pl.ds(pl.multiple_of(i * step, step), step)
            hit = (iota((step, entries), 0) + i * step) == item
            b_one[at, :] = jnp.where(hit, 1.0, 0.0).astype(BF16)
            b_hi[at, :] = jnp.where(hit, rate_top, 0.0).astype(BF16)
            b_lo[at, :] = jnp.where(hit, rate_low, 0.0).astype(BF16)
            return 0

        lax.fori_loop(0, items // step, body, 0)

    def counts_and_ratings(t):
        pos = pos_tab[t : t + 1, :]

        def body(i, _):
            at = pl.ds(pl.multiple_of(i * RUN, RUN), RUN)
            here = (iota((RUN, entries), 0) + i * RUN).astype(F32)
            hot = onehot(here == pos)
            num[at, :] = mm(hot, b_one[...], NT)
            rat[at, :] = mm(hot, b_hi[...], NT) + mm(hot, b_lo[...], NT)
            return 0

        lax.fori_loop(0, GROUPS, body, 0)

    def split_v():
        top, low = halves(v_cur[...])
        v_hi[...] = top
        v_lo[...] = low

    load_v.wait()
    split_v()
    one_hot_items(0)

    def select_rows(t):
        mask = mask_recv[:, t, :]
        before = onehot(iota((RUN, RUN), 0) < iota((RUN, RUN), 1))
        rank = mm(mask.astype(BF16), before, NN)
        spread = onehot(iota((OWNERS * TOUCH, OWNERS), 0) // TOUCH == iota((OWNERS * TOUCH, OWNERS), 1))
        rank_rows = mm(spread, rank.astype(BF16), NN)
        mask_rows = mm(spread, mask.astype(BF16), NN)
        index = (iota((OWNERS * TOUCH, RUN), 0) % TOUCH).astype(F32)
        hit = jnp.where(rank_rows == index, mask_rows, 0.0)
        sel[t] = hit.astype(BF16)
        sel_t[t] = hit.T.astype(BF16)

    def send_rows(t):
        for group in ORDER:
            hot = sel[t, rows_of(group), :]
            rows = mm(hot, u_parts[0], NN) + mm(hot, u_parts[1], NN)
            for slot in slots_of(group):
                part = rows[(slot % SIDE) * TOUCH : (slot % SIDE + 1) * TOUCH, :]
                if slot:
                    u_send[t, slot] = part
                else:
                    u_recv[t, slot] = part
            for slot in slots_of(group):
                if slot:
                    u_copy(t, slot).start()

    def tile_rows(t):
        for group in ORDER:
            for slot in slots_of(group):
                if slot:
                    u_copy(t, slot).wait_recv()
            at = rows_of(group)
            top, low = halves(u_recv[t, group * SIDE : (group + 1) * SIDE].reshape(RUN, -1))
            ut_hi[at, :] = top
            ut_lo[at, :] = low
            v = (v_hi[...], v_lo[...])
            w = rat[at, :] - num[at, :] * mm3((top, low), v, NT)
            w_top, w_low = halves(w)
            w_hi[at, :] = w_top
            w_lo[at, :] = w_low
            grad = mm3((w_top, w_low), v, NN)
            for slot in slots_of(group):
                part = grad[(slot % SIDE) * TOUCH : (slot % SIDE + 1) * TOUCH, :]
                if slot:
                    g_send[t, slot] = part
                else:
                    g_recv[t, slot] = part
            for slot in slots_of(group):
                if slot:
                    g_copy(t, slot).start()

    def item_step(t):
        step = steps_of(t)

        def body(i, _):
            at = pl.ds(pl.multiple_of(i * RUN, RUN), RUN)
            grad = mm3((w_hi[:, at], w_lo[:, at]), (ut_hi[...], ut_lo[...]), TN)
            v_new[t, at, :] = v_cur[at, :] + step * (grad - 0.1 * v_cur[at, :])
            return 0

        lax.fori_loop(0, items // RUN, body, 0)

    def user_step(t):
        total = jnp.zeros_like(u_own[...])
        for group in ORDER:
            for slot in slots_of(group):
                if slot:
                    g_copy(t, slot).wait_recv()
            top, low = halves(g_recv[t, group * SIDE : (group + 1) * SIDE].reshape(RUN, -1))
            back = sel_t[t, :, rows_of(group)]
            total = total + mm(back, top, NN) + mm(back, low, NN)
        old = u_own[...]
        return old + steps_of(t) * (total - 0.1 * old)


    for slot in range(1, OWNERS):
        mask_copy(slot).wait_recv()
    select_rows(0)
    send_rows(0)
    counts_and_ratings(0)
    tile_rows(0)
    item_step(0)
    v_first = pltpu.make_async_remote_copy(
        src_ref=v_new.at[0], dst_ref=v_new.at[1],
        send_sem=v_ss.at[0], recv_sem=v_rs.at[0],
        device_id=(up, place), device_id_type=MESH)
    v_first.start()
    select_rows(1)
    one_hot_items(1)
    counts_and_ratings(1)
    fresh = user_step(0)
    u_own[...] = fresh
    top, low = halves(fresh)
    u_parts[0] = top
    u_parts[1] = low
    send_rows(1)
    v_first.wait()
    v_cur[...] = v_new[1]
    split_v()
    tile_rows(1)
    item_step(1)
    v_last = pltpu.make_async_remote_copy(
        src_ref=v_new.at[1], dst_ref=out_v,
        send_sem=v_ss.at[1], recv_sem=v_rs.at[1],
        device_id=(down, place), device_id_type=MESH)
    v_last.start()
    out_u[...] = user_step(1)
    for slot in range(1, OWNERS):
        mask_copy(slot).wait_send()
        for t in range(subs):
            u_copy(t, slot).wait_send()
            g_copy(t, slot).wait_send()
    v_last.wait()


def on_device(n_rows, user_factors, item_factors, ratings, user_offsets, item_offsets, counts):
    users, rank = user_factors.shape
    items = item_factors.shape[0]
    subs, entries = ratings.shape
    picked = OWNERS * TOUCH
    vmem = pl.BlockSpec(memory_space=pltpu.VMEM)
    hbm = pl.BlockSpec(memory_space=pl.ANY)
    dma = pltpu.SemaphoreType.DMA
    return pl.pallas_call(
        functools.partial(kernel, n_rows),
        out_shape=(
            jax.ShapeDtypeStruct((users, rank), F32),
            jax.ShapeDtypeStruct((items, rank), F32),
        ),
        in_specs=[hbm, hbm, vmem, vmem, vmem, vmem],
        out_specs=(vmem, vmem),
        scratch_shapes=[
            pltpu.VMEM((users, rank), F32),
            pltpu.VMEM((items, rank), F32),
            pltpu.VMEM((subs, items, rank), F32),
            pltpu.VMEM((items, rank), BF16),
            pltpu.VMEM((items, rank), BF16),
            pltpu.VMEM((OWNERS, 8, RUN), F32),
            pltpu.VMEM((OWNERS, 8, RUN), F32),
            pltpu.VMEM((8, 128), F32),
            pltpu.VMEM((8, entries), F32),
            pltpu.VMEM((subs, picked, RUN), BF16),
            pltpu.VMEM((subs, RUN, picked), BF16),
            pltpu.VMEM((items, entries), BF16),
            pltpu.VMEM((items, entries), BF16),
            pltpu.VMEM((items, entries), BF16),
            pltpu.VMEM((picked, items), F32),
            pltpu.VMEM((picked, items), F32),
            pltpu.VMEM((picked, rank), BF16),
            pltpu.VMEM((picked, rank), BF16),
            pltpu.VMEM((picked, items), BF16),
            pltpu.VMEM((picked, items), BF16),
            pltpu.VMEM((subs, OWNERS, TOUCH, rank), F32),
            pltpu.VMEM((subs, OWNERS, TOUCH, rank), F32),
            pltpu.VMEM((subs, OWNERS, TOUCH, rank), F32),
            pltpu.VMEM((subs, OWNERS, TOUCH, rank), F32),
            pltpu.VMEM((2, users, rank), BF16),
            dma((2,)),
            dma((OWNERS,)),
            dma((OWNERS,)),
            dma((subs, OWNERS)),
            dma((subs, OWNERS)),
            dma((subs, OWNERS)),
            dma((subs, OWNERS)),
            dma((2,)),
            dma((2,)),
        ],
        compiler_params=pltpu.CompilerParams(
            collective_id=0, has_side_effects=True, vmem_limit_bytes=56 * 1024 * 1024
        ),
        name="sgd",
    )(user_factors, item_factors, ratings, user_offsets, item_offsets, counts)


def solution(mesh):
    shard = P(("rows", "strata"), None)
    split = P(None, ("rows", "strata"))
    return jax.shard_map(
        functools.partial(on_device, mesh.shape["rows"]),
        mesh=mesh,
        in_specs=(shard, shard, split, split, split, split),
        out_specs=(shard, shard),
        check_vma=False,
    )
```

time: 342 us -> 85.6 us (0.25)
  the two profiles are of different devices: /device:TPU:96 before, /device:TPU:73 now
where the time goes in v1:
time: 85.6 us; the launch traced here: 85.4 us
  Pallas kernels  79.6 us (93%)
  local copies, waits for them, and re-layouts  5.23 us (6%)
    pallas_call x1, Pallas kernels, on_device(): pl.pallas_call(functools.partial(kernel, n_rows), out_shape=(jax.ShapeDty...  79.6 us
    unnamed x3, local copies, waits for them, and re-layouts  5.23 us

profile of v1, /device:TPU:73, one launch (start us, length us, event | category | flops | bytes accessed | tf_op | source)
XLA Modules:
  0.0 85.4 jit_solution(572948098007654259)
XLA Ops:
  0.6 1.3 %copy.8.count_ref = s32[2,1]{1,0:T(2,128)} copy(s32[2,1]{0,1:T(1,128)} %param.11) | data formatting | bytes 16 | tf_op args[5]
  1.9 79.6 %sgd.1 = (f32[128,512]{1,0:T(8,128)}, f32[512,512]{1,0:T(8,128)}) custom-call(f32[128,512]{1,0:T(8,128)} %u_hbm.1, f32[512,512]{1,0:T(8,128)} %v_hbm.1, f32[2,1024]{1,0:T(2,128)} %rate_ref.1, s32[2,1024]{1,0:T(2,128)} %user_ref.1, s32[2,1024]{1,0:T(2,128)} %item_ref.1, s32[2,1]{1,0:T(2,128)} %copy.8.count_ref), custom_call_target="tpu_custom_call" | custom-call | tf_op jit(solution)/shard_map/sgd/pallas_call | solution.py:311
  81.5 1.7 %copy.11 = f32[128,512]{1,0:T(8,128)} copy(f32[128,512]{1,0:T(8,128)} %get-tuple-element.4) | data formatting | bytes 524288
  83.2 2.3 %copy.12 = f32[512,512]{1,0:T(8,128)} copy(f32[512,512]{1,0:T(8,128)} %get-tuple-element.5) | data formatting | bytes 2097152

commit v2 on v1

--- a/solution.py
+++ b/solution.py
@@ -16,7 +16,7 @@
 RUN = 128
 TOUCH = 32
 GROUPS = SIDE
-ORDER = (0, 1, 3, 2)
+STEPS = (0, 1, 3, 2)
 
 NN = (((1,), (0,)), ((), ()))
 NT = (((1,), (1,)), ((), ()))
@@ -52,7 +52,7 @@
     n_rows,
     u_hbm, v_hbm, rate_ref, user_ref, item_ref, count_ref,
     out_u, out_v,
-    u_own, v_cur, v_new, v_hi, v_lo,
+    u_own, v_cur, v_in, v_new, v_hi, v_lo,
     mask_send, mask_recv, rank_tab, pos_tab,
     sel, sel_t,
     b_one, b_hi, b_lo, num, rat,
@@ -69,7 +69,7 @@
     subs = rate_ref.shape[0]
 
     def away(slot, sign):
-        dy, dx = slot // SIDE, slot % SIDE
+        dy, dx = STEPS[slot // SIDE], slot % SIDE
         return ((y + sign * dy + SIDE) % SIDE) * SIDE + (x + sign * dx + SIDE) % SIDE
 
     def tile_of(slot):
@@ -94,7 +94,7 @@
         owner = user >> 7
         dy = (y + SIDE - (owner >> 2)) & 3
         dx = (x + SIDE - (owner & 3)) & 3
-        return dy * SIDE + dx, user & (RUN - 1)
+        return (dy ^ (dy >> 1)) * SIDE + dx, user & (RUN - 1)
 
     for t in range(subs):
         slot_e, low_e = slot_and_run(t)
@@ -113,20 +113,35 @@
     def mask_copy(slot):
         return pltpu.make_async_remote_copy(
             src_ref=mask_send.at[slot], dst_ref=mask_recv.at[slot],
-            send_sem=mask_ss.at[slot], recv_sem=mask_rs.at[slot],
+            send_sem=mask_ss, recv_sem=mask_rs,
             device_id=owner_of(slot), device_id_type=MESH)
 
-    def u_copy(t, slot):
+    cut = u_own.shape[1] // 2
+    WHOLE = slice(0, 2 * cut)
+    HALVES = (slice(0, cut), slice(cut, 2 * cut))
+
+    def parts_of(split):
+        return HALVES if split else (WHOLE,)
+
+    def u_copy(t, slot, cols):
+        part = 1 if cols.start else 0
         return pltpu.make_async_remote_copy(
-            src_ref=u_send.at[t, slot], dst_ref=u_recv.at[t, slot],
-            send_sem=u_ss.at[t, slot], recv_sem=u_rs.at[t, slot],
+            src_ref=u_send.at[t, slot, :, cols], dst_ref=u_recv.at[t, slot, :, cols],
+            send_sem=u_ss, recv_sem=u_rs.at[t, part, slot // SIDE],
             device_id=tile_of(slot), device_id_type=MESH)
 
-    def g_copy(t, slot):
+    def g_copy(t, slot, cols):
+        part = 1 if cols.start else 0
         return pltpu.make_async_remote_copy(
-            src_ref=g_send.at[t, slot], dst_ref=g_recv.at[t, slot],
-            send_sem=g_ss.at[t, slot], recv_sem=g_rs.at[t, slot],
+            src_ref=g_send.at[t, slot, :, cols], dst_ref=g_recv.at[t, slot, :, cols],
+            send_sem=g_ss, recv_sem=g_rs.at[t, part, slot // SIDE],
             device_id=owner_of(slot), device_id_type=MESH)
+
+    def arrived(recv, sems, t, group, cols):
+        first = max(1, group * SIDE)
+        part = recv.at[t, first : (group + 1) * SIDE, :, cols]
+        sem = sems.at[t, 1 if cols.start else 0, group]
+        pltpu.make_async_copy(part, part, sem).wait()
 
     def slots_of(group):
         return range(group * SIDE, (group + 1) * SIDE)
@@ -134,7 +149,7 @@
     def rows_of(group):
         return slice(group * RUN, (group + 1) * RUN)
 
-    for group in ORDER:
+    for group in range(GROUPS):
         for slot in slots_of(group):
             if slot:
                 mask_copy(slot).start()
@@ -146,7 +161,7 @@
     u_parts[1] = low
 
     def one_hot_items(t):
-        active = iota((1, entries), 1) < count_ref[t : t + 1, 0:1]
+        active = iota((1, entries), 1) < count_ref[0:1, t : t + 1]
         rate = rate_ref[t : t + 1, :]
         rate_top = rate.astype(BF16).astype(F32)
         rate_low = rate - rate_top
@@ -170,8 +185,8 @@
             at = pl.ds(pl.multiple_of(i * RUN, RUN), RUN)
             here = (iota((RUN, entries), 0) + i * RUN).astype(F32)
             hot = onehot(here == pos)
-            num[at, :] = mm(hot, b_one[...], NT)
-            rat[at, :] = mm(hot, b_hi[...], NT) + mm(hot, b_lo[...], NT)
+            num[t, at, :] = mm(hot, b_one[...], NT)
+            rat[t, at, :] = mm(hot, b_hi[...], NT) + mm(hot, b_lo[...], NT)
             return 0
 
         lax.fori_loop(0, GROUPS, body, 0)
@@ -183,7 +198,6 @@
 
     load_v.wait()
     split_v()
-    one_hot_items(0)
 
     def select_rows(t):
         mask = mask_recv[:, t, :]
@@ -197,31 +211,37 @@
         sel[t] = hit.astype(BF16)
         sel_t[t] = hit.T.astype(BF16)
 
-    def send_rows(t):
-        for group in ORDER:
+    def send_rows(t, cols):
+        for group in range(GROUPS):
             hot = sel[t, rows_of(group), :]
-            rows = mm(hot, u_parts[0], NN) + mm(hot, u_parts[1], NN)
+            rows = mm(hot, u_parts[0, :, cols], NN) + mm(hot, u_parts[1, :, cols], NN)
             for slot in slots_of(group):
                 part = rows[(slot % SIDE) * TOUCH : (slot % SIDE + 1) * TOUCH, :]
                 if slot:
-                    u_send[t, slot] = part
+                    u_send[t, slot, :, cols] = part
                 else:
-                    u_recv[t, slot] = part
+                    u_recv[t, slot, :, cols] = part
             for slot in slots_of(group):
                 if slot:
-                    u_copy(t, slot).start()
-
-    def tile_rows(t):
-        for group in ORDER:
-            for slot in slots_of(group):
-                if slot:
-                    u_copy(t, slot).wait_recv()
+                    u_copy(t, slot, cols).start()
+
+    def tile_rows(t, u_split, g_split):
+        held = []
+        for group in range(GROUPS):
+            if group == GROUPS - 1:
+                item_begin(t)
+            for cols in parts_of(u_split):
+                arrived(u_recv, u_rs, t, group, cols)
+            if t + 1 == subs and group == GROUPS - 1:
+                for slot, cols in held:
+                    g_copy(t, slot, cols).start()
+                held = []
             at = rows_of(group)
             top, low = halves(u_recv[t, group * SIDE : (group + 1) * SIDE].reshape(RUN, -1))
             ut_hi[at, :] = top
             ut_lo[at, :] = low
             v = (v_hi[...], v_lo[...])
-            w = rat[at, :] - num[at, :] * mm3((top, low), v, NT)
+            w = rat[t, at, :] - num[t, at, :] * mm3((top, low), v, NT)
             w_top, w_low = halves(w)
             w_hi[at, :] = w_top
             w_lo[at, :] = w_low
@@ -232,72 +252,95 @@
                     g_send[t, slot] = part
                 else:
                     g_recv[t, slot] = part
-            for slot in slots_of(group):
-                if slot:
-                    g_copy(t, slot).start()
+            last_group = group == GROUPS - 1
+            for part, cols in enumerate(parts_of(g_split)):
+                for slot in slots_of(group):
+                    if slot:
+                        if not last_group and (part or t + 1 == subs):
+                            held.append((slot, cols))
+                        elif not part:
+                            g_copy(t, slot, cols).start()
+                        else:
+                            held.append((slot, cols))
+        for slot, cols in held:
+            g_copy(t, slot, cols).start()
+
+    def user_step(t, cols):
+        old = u_own[:, cols]
+        total = jnp.zeros_like(old)
+        for group in range(GROUPS):
+            arrived(g_recv, g_rs, t, group, cols)
+            top, low = halves(g_recv[t, group * SIDE : (group + 1) * SIDE, :, cols].reshape(RUN, -1))
+            back = sel_t[t, :, rows_of(group)]
+            total = total + mm(back, top, NN) + mm(back, low, NN)
+        u_own[:, cols] = old + steps_of(t) * (total - 0.1 * old)
+
+    def update_half(t, cols):
+        user_step(t, cols)
+        top, low = halves(u_own[:, cols])
+        u_parts[0, :, cols] = top
+        u_parts[1, :, cols] = low
+        send_rows(t + 1, cols)
+
+    def v_copy(t, chunk):
+        at = pl.ds(chunk * RUN, RUN)
+        dst = out_v if t + 1 == subs else v_in
+        return pltpu.make_async_remote_copy(
+            src_ref=v_new.at[t, at], dst_ref=dst.at[at],
+            send_sem=v_ss, recv_sem=v_rs.at[t],
+            device_id=(down if t + 1 == subs else up, place), device_id_type=MESH)
+
+    def item_grad(t, first, last, chunk):
+        at = slice(chunk * RUN, (chunk + 1) * RUN)
+        rows = slice(first * RUN, last * RUN)
+        return mm3((w_hi[rows, at], w_lo[rows, at]), (ut_hi[rows, :], ut_lo[rows, :]), TN)
+
+    def item_begin(t):
+        for chunk in range(items // RUN):
+            v_new[t, chunk * RUN : (chunk + 1) * RUN, :] = item_grad(t, 0, GROUPS - 1, chunk)
 
     def item_step(t):
         step = steps_of(t)
-
-        def body(i, _):
-            at = pl.ds(pl.multiple_of(i * RUN, RUN), RUN)
-            grad = mm3((w_hi[:, at], w_lo[:, at]), (ut_hi[...], ut_lo[...]), TN)
+        for chunk in range(items // RUN):
+            at = slice(chunk * RUN, (chunk + 1) * RUN)
+            grad = v_new[t, at, :] + item_grad(t, GROUPS - 1, GROUPS, chunk)
             v_new[t, at, :] = v_cur[at, :] + step * (grad - 0.1 * v_cur[at, :])
-            return 0
-
-        lax.fori_loop(0, items // RUN, body, 0)
-
-    def user_step(t):
-        total = jnp.zeros_like(u_own[...])
-        for group in ORDER:
-            for slot in slots_of(group):
-                if slot:
-                    g_copy(t, slot).wait_recv()
-            top, low = halves(g_recv[t, group * SIDE : (group + 1) * SIDE].reshape(RUN, -1))
-            back = sel_t[t, :, rows_of(group)]
-            total = total + mm(back, top, NN) + mm(back, low, NN)
-        old = u_own[...]
-        return old + steps_of(t) * (total - 0.1 * old)
-
-
-    for slot in range(1, OWNERS):
-        mask_copy(slot).wait_recv()
+            v_copy(t, chunk).start()
+
+    one_hot_items(0)
+    counts_and_ratings(0)
+    def wait_masks():
+        pltpu.make_async_copy(mask_recv.at[1:OWNERS], mask_recv.at[1:OWNERS], mask_rs).wait()
+
+    wait_masks()
     select_rows(0)
-    send_rows(0)
-    counts_and_ratings(0)
-    tile_rows(0)
-    item_step(0)
-    v_first = pltpu.make_async_remote_copy(
-        src_ref=v_new.at[0], dst_ref=v_new.at[1],
-        send_sem=v_ss.at[0], recv_sem=v_rs.at[0],
-        device_id=(up, place), device_id_type=MESH)
-    v_first.start()
+    send_rows(0, WHOLE)
     select_rows(1)
     one_hot_items(1)
     counts_and_ratings(1)
-    fresh = user_step(0)
-    u_own[...] = fresh
-    top, low = halves(fresh)
-    u_parts[0] = top
-    u_parts[1] = low
-    send_rows(1)
-    v_first.wait()
-    v_cur[...] = v_new[1]
+    tile_rows(0, False, False)
+    item_step(0)
+    update_half(0, WHOLE)
+
+    def wait_v():
+        pltpu.make_async_copy(v_in, v_in, v_rs.at[0]).wait()
+
+    wait_v()
+    v_cur[...] = v_in[...]
     split_v()
-    tile_rows(1)
+    tile_rows(1, False, False)
     item_step(1)
-    v_last = pltpu.make_async_remote_copy(
-        src_ref=v_new.at[1], dst_ref=out_v,
-        send_sem=v_ss.at[1], recv_sem=v_rs.at[1],
-        device_id=(down, place), device_id_type=MESH)
-    v_last.start()
-    out_u[...] = user_step(1)
-    for slot in range(1, OWNERS):
-        mask_copy(slot).wait_send()
-        for t in range(subs):
-            u_copy(t, slot).wait_send()
-            g_copy(t, slot).wait_send()
-    v_last.wait()
+    user_step(1, WHOLE)
+    put_u = pltpu.make_async_copy(u_own, out_u, load_sem.at[0])
+    put_u.start()
+    def finish():
+        for sent, sem in ((mask_send.at[1:OWNERS], mask_ss), (u_send.at[:, 1:OWNERS], u_ss), (g_send.at[:, 1:OWNERS], g_ss)):
+            pltpu.make_async_copy(sent, sent, sem).wait()
+        pltpu.make_async_copy(v_new, v_new, v_ss).wait()
+        pltpu.make_async_copy(out_v, out_v, v_rs.at[1]).wait()
+        put_u.wait()
+
+    finish()
 
 
 def on_device(n_rows, user_factors, item_factors, ratings, user_offsets, item_offsets, counts):
@@ -311,13 +354,14 @@
     return pl.pallas_call(
         functools.partial(kernel, n_rows),
         out_shape=(
-            jax.ShapeDtypeStruct((users, rank), F32),
-            jax.ShapeDtypeStruct((items, rank), F32),
+            pltpu.VMEM((users, rank), F32),
+            pltpu.VMEM((items, rank), F32),
         ),
         in_specs=[hbm, hbm, vmem, vmem, vmem, vmem],
-        out_specs=(vmem, vmem),
+        out_specs=(hbm, hbm),
         scratch_shapes=[
             pltpu.VMEM((users, rank), F32),
+            pltpu.VMEM((items, rank), F32),
             pltpu.VMEM((items, rank), F32),
             pltpu.VMEM((subs, items, rank), F32),
             pltpu.VMEM((items, rank), BF16),
@@ -331,8 +375,8 @@
             pltpu.VMEM((items, entries), BF16),
             pltpu.VMEM((items, entries), BF16),
             pltpu.VMEM((items, entries), BF16),
-            pltpu.VMEM((picked, items), F32),
-            pltpu.VMEM((picked, items), F32),
+            pltpu.VMEM((subs, picked, items), F32),
+            pltpu.VMEM((subs, picked, items), F32),
             pltpu.VMEM((picked, rank), BF16),
             pltpu.VMEM((picked, rank), BF16),
             pltpu.VMEM((picked, items), BF16),
@@ -343,20 +387,20 @@
             pltpu.VMEM((subs, OWNERS, TOUCH, rank), F32),
             pltpu.VMEM((2, users, rank), BF16),
             dma((2,)),
-            dma((OWNERS,)),
-            dma((OWNERS,)),
-            dma((subs, OWNERS)),
-            dma((subs, OWNERS)),
-            dma((subs, OWNERS)),
-            dma((subs, OWNERS)),
-            dma((2,)),
-            dma((2,)),
+            dma,
+            dma,
+            dma,
+            dma((subs, 2, GROUPS)),
+            dma,
+            dma((subs, 2, GROUPS)),
+            dma,
+            dma((subs,)),
         ],
         compiler_params=pltpu.CompilerParams(
             collective_id=0, has_side_effects=True, vmem_limit_bytes=56 * 1024 * 1024
         ),
         name="sgd",
-    )(user_factors, item_factors, ratings, user_offsets, item_offsets, counts)
+    )(user_factors, item_factors, ratings, user_offsets, item_offsets, counts.T)
 
 
 def solution(mesh):

time: 85.6 us -> 76.8 us (0.90)
  the two profiles are of different devices: /device:TPU:73 before, /device:TPU:96 now
where the time goes in v2:
time: 76.8 us; the launch traced here: 75.6 us
  Pallas kernels  73.2 us (95%)
  local copies, waits for them, and re-layouts  1.67 us (2%)
    pallas_call x1, Pallas kernels, on_device(): pl.pallas_call(functools.partial(kernel, n_rows), out_shape=(pltpu.VMEM((...  73.2 us
    unnamed x2, local copies, waits for them, and re-layouts  1.67 us

profile of v2, /device:TPU:96, one launch (start us, length us, event | category | flops | bytes accessed | tf_op | source)
XLA Modules:
  0.0 75.6 jit_solution(15744373451282216701)
XLA Ops:
  0.6 73.2 %sgd.1 = (f32[128,512]{1,0:T(8,128)S(1)}, f32[512,512]{1,0:T(8,128)S(1)}) custom-call(f32[128,512]{1,0:T(8,128)} %u_hbm.1, f32[512,512]{1,0:T(8,128)} %v_hbm.1, f32[2,1024]{1,0:T(2,128)} %rate_ref.1, s32[2,1024]{1,0:T(2,128)} %user_ref.1, s32[2,1024]{1,0:T(2,128)} %item_ref.1, s32[1,2]{1,0:T(1,128)} %bitcast.1), custom_call_target="tpu_custom_call" | custom-call | tf_op jit(solution)/shard_map/sgd/pallas_call | solution.py:354
  73.9 0.7 copy.10
  74.6 1.0 %copy.11 = f32[512,512]{1,0:T(8,128)} copy(f32[512,512]{1,0:T(8,128)S(1)} %get-tuple-element.3) | data formatting | bytes 2097152

commit v3 on v2

v3 whole, which is shorter than its diff:
```python
import functools

import jax
import jax.numpy as jnp
from jax import lax
from jax.experimental import pallas as pl
from jax.experimental.pallas import tpu as pltpu
from jax.sharding import PartitionSpec as P

MESH = pl.DeviceIdType.MESH
F32 = jnp.float32
BF16 = jnp.bfloat16

SIDE = 4
OWNERS = SIDE * SIDE
RUN = 128
TOUCH = 32
GROUPS = SIDE
STEPS = (0, 1, 3, 2)

NN = (((1,), (0,)), ((), ()))
NT = (((1,), (1,)), ((), ()))
TN = (((0,), (0,)), ((), ()))


def mm(a, b, dims):
    return lax.dot_general(a, b, dims, preferred_element_type=F32)


def halves(value):
    top = value.astype(BF16)
    return top, (value - top.astype(F32)).astype(BF16)


def mm3(a, b, dims):
    return mm(a[0], b[0], dims) + mm(a[0], b[1], dims) + mm(a[1], b[0], dims)


def iota(shape, dim):
    return lax.broadcasted_iota(jnp.int32, shape, dim)


def onehot(test):
    return jnp.where(test, 1.0, 0.0).astype(BF16)


def steps_of(sub_epoch):
    return 0.04 / (1.0 + 0.5 * sub_epoch)


def kernel(
    n_rows,
    u_hbm, v_hbm, rate_ref, user_ref, item_ref, count_ref,
    out_u, out_v,
    u_own, v_cur, v_in, v_new, v_hi, v_lo,
    mask_send, mask_recv, rank_tab, pos_tab,
    sel, sel_t,
    b_one, b_hi, b_lo, num, rat,
    ut_hi, ut_lo, w_hi, w_lo,
    u_send, u_recv, g_send, g_recv, u_parts,
    relay_mask, dense, relay_send,
    pack_send, pack_recv, away_rows, own_hi, own_lo,
    pack_ss, pack_rs, away_ss, away_rs,
    dense_ss, relay_ss, relay_ms, relay_mrs, dense_rs, relay_rs,
    load_sem, mask_ss, mask_rs, u_ss, u_rs, g_ss, g_rs, v_ss, v_rs,
):
    row = lax.axis_index("rows")
    place = lax.axis_index("strata")
    y, x = place // SIDE, place % SIDE
    up, down = (row + 1) % n_rows, (row + n_rows - 1) % n_rows
    items = v_cur.shape[0]
    entries = rate_ref.shape[1]
    subs = rate_ref.shape[0]

    def away(slot, sign):
        dy, dx = STEPS[slot // SIDE], slot % SIDE
        return ((y + sign * dy + SIDE) % SIDE) * SIDE + (x + sign * dx + SIDE) % SIDE

    def tile_of(slot):
        return (row, away(slot, 1))

    def owner_of(slot):
        return (row, away(slot, -1))

    barrier = pltpu.get_barrier_semaphore()
    for slot in range(1, OWNERS):
        pl.semaphore_signal(barrier, inc=1, device_id=tile_of(slot), device_id_type=MESH)
    for other in (up, down):
        pl.semaphore_signal(barrier, inc=1, device_id=(other, place), device_id_type=MESH)

    load_u = pltpu.make_async_copy(u_hbm, u_own, load_sem.at[0])
    load_v = pltpu.make_async_copy(v_hbm, v_cur, load_sem.at[1])
    load_u.start()
    load_v.start()

    def slot_and_run(t):
        user = user_ref[t : t + 1, :]
        owner = user >> 7
        dy = (y + SIDE - (owner >> 2)) & 3
        dx = (x + SIDE - (owner & 3)) & 3
        return (dy ^ (dy >> 1)) * SIDE + dx, user & (RUN - 1)

    for t in range(subs):
        slot_e, low_e = slot_and_run(t)
        hot_slot = onehot(iota((OWNERS, entries), 0) == slot_e)
        hot_low = onehot(iota((RUN, entries), 0) == low_e)
        named = jnp.where(mm(hot_slot, hot_low, NT) > 0.5, 1.0, 0.0)
        mask_send[:, :, t, :] = named.reshape(GROUPS, SIDE, RUN)
        before = onehot(iota((RUN, RUN), 0) < iota((RUN, RUN), 1))
        rank = mm(named.astype(BF16), before, NN)
        each = mm(rank.astype(BF16), hot_low, NN)
        rank_e = jnp.sum(jnp.where(iota((OWNERS, entries), 0) == slot_e, each, 0.0), axis=0, keepdims=True)
        pos_tab[t : t + 1, :] = slot_e.astype(F32) * float(TOUCH) + rank_e

    pack_send[0:1, :] = pos_tab[subs - 1 : subs, :]
    pack_send[1:2, :] = jnp.where(
        iota((1, entries), 1) < count_ref[0:1, subs - 1 : subs], item_ref[subs - 1 : subs, :], -1
    ).astype(F32)
    pack_send[2:3, :] = rate_ref[subs - 1 : subs, :]
    pl.semaphore_wait(barrier, OWNERS + 1)

    def mask_copy(slot):
        return pltpu.make_async_remote_copy(
            src_ref=mask_send.at[slot // SIDE, slot % SIDE], dst_ref=mask_recv.at[slot],
            send_sem=mask_ss, recv_sem=mask_rs,
            device_id=owner_of(slot), device_id_type=MESH)

    cut = u_own.shape[1] // 2
    HALVES = (slice(0, cut), slice(cut, 2 * cut))

    def u_copy(slot):
        return pltpu.make_async_remote_copy(
            src_ref=u_send.at[slot], dst_ref=u_recv.at[1, slot // SIDE, slot % SIDE],
            send_sem=u_ss, recv_sem=u_rs.at[slot // SIDE],
            device_id=tile_of(slot), device_id_type=MESH)

    def g_copy(t, slot):
        return pltpu.make_async_remote_copy(
            src_ref=g_send.at[t, slot], dst_ref=g_recv.at[t, slot],
            send_sem=g_ss, recv_sem=g_rs.at[t, slot // SIDE],
            device_id=owner_of(slot), device_id_type=MESH)

    def rows_in(t, group):
        if t:
            all_in(u_recv.at[t, group, (1 if group == 0 else 0) :], u_rs.at[group])
            return
        if group == 0:
            for step in range(1, SIDE):
                all_in(u_recv.at[0, :, step, :, HALVES[1]], relay_rs.at[1, step])
        else:
            all_in(u_recv.at[0, group, :, :, HALVES[0]], relay_rs.at[0, group])

    def grads_in(t, group):
        first = max(1, group * SIDE)
        all_in(g_recv.at[t, first : (group + 1) * SIDE], g_rs.at[t, group])

    def slots_of(group):
        return range(group * SIDE, (group + 1) * SIDE)

    def rows_of(group):
        return slice(group * RUN, (group + 1) * RUN)

    def named_items(t):
        active = iota((1, entries), 1) < count_ref[0:1, t : t + 1]
        return jnp.where(active, item_ref[t : t + 1, :], -1).astype(F32)

    def one_hot_items(t):
        if t < subs:
            rate, item = rate_ref[t : t + 1, :], named_items(t)
        else:
            rate, item = pack_recv[2:3, :], pack_recv[1:2, :]
        rate_top = rate.astype(BF16).astype(F32)
        rate_low = rate - rate_top
        step = 64

        def body(i, _):
            at = pl.ds(pl.multiple_of(i * step, step), step)
            hit = (iota((step, entries), 0) + i * step).astype(F32) == item
            b_one[at, :] = jnp.where(hit, 1.0, 0.0).astype(BF16)
            b_hi[at, :] = jnp.where(hit, rate_top, 0.0).astype(BF16)
            b_lo[at, :] = jnp.where(hit, rate_low, 0.0).astype(BF16)
            return 0

        lax.fori_loop(0, items // step, body, 0)

    def counts_and_ratings(t):
        pos = pos_tab[t : t + 1, :] if t < subs else pack_recv[0:1, :]

        def body(i, _):
            at = pl.ds(pl.multiple_of(i * RUN, RUN), RUN)
            here = (iota((RUN, entries), 0) + i * RUN).astype(F32)
            hot = onehot(here == pos)
            num[t, at, :] = mm(hot, b_one[...], NT)
            rat[t, at, :] = mm(hot, b_hi[...], NT) + mm(hot, b_lo[...], NT)
            return 0

        lax.fori_loop(0, GROUPS, body, 0)

    def split_v():
        top, low = halves(v_cur[...])
        v_hi[...] = top
        v_lo[...] = low


    def relay_place(hop, step, sign):
        dy, dx = (0, step) if hop == 0 else (STEPS[step], 0)
        return (row, ((y + sign * dy + SIDE) % SIDE) * SIDE + (x + sign * dx + SIDE) % SIDE)

    def dense_copy(hop, step):
        return pltpu.make_async_remote_copy(
            src_ref=u_own.at[:, HALVES[hop]], dst_ref=dense.at[hop, step],
            send_sem=dense_ss, recv_sem=dense_rs.at[hop],
            device_id=relay_place(hop, step, 1), device_id_type=MESH)

    def relay_mask_copy(hop, step):
        src = mask_send.at[step] if hop == 0 else mask_send.at[:, step]
        return pltpu.make_async_remote_copy(
            src_ref=src, dst_ref=relay_mask.at[hop, step],
            send_sem=relay_ms, recv_sem=relay_mrs.at[hop],
            device_id=relay_place(1 - hop, step, -1), device_id_type=MESH)

    def relay_copy(hop, step):
        cols = HALVES[hop]
        dst = u_recv.at[0, step, :, :, cols] if hop == 0 else u_recv.at[0, :, step, :, cols]
        return pltpu.make_async_remote_copy(
            src_ref=relay_send.at[hop, step], dst_ref=dst,
            send_sem=relay_ss, recv_sem=relay_rs.at[hop, step],
            device_id=relay_place(1 - hop, step, 1), device_id_type=MESH)

    def all_in(part, sem):
        pltpu.make_async_copy(part, part, sem).wait()

    def relay_out(hop):
        all_in(relay_mask.at[hop, 1:SIDE], relay_mrs.at[hop])
        if hop == 0:
            relay_mask[hop, 0] = mask_send[0]
        else:
            relay_mask[hop, 0] = mask_send[:, 0]
        mask = relay_mask[hop, :, :, 0, :].reshape(OWNERS, RUN)
        before = onehot(iota((RUN, RUN), 0) < iota((RUN, RUN), 1))
        rank = mm(mask.astype(BF16), before, NN)
        line = iota((OWNERS * TOUCH, OWNERS), 0)
        spread = onehot((line // TOUCH % SIDE) * SIDE + line // RUN == iota((OWNERS * TOUCH, OWNERS), 1))
        rank_rows = mm(spread, rank.astype(BF16), NN)
        mask_rows = mm(spread, mask.astype(BF16), NN)
        index = (iota((OWNERS * TOUCH, RUN), 0) % TOUCH).astype(F32)
        hit = jnp.where(rank_rows == index, mask_rows, 0.0).astype(BF16)
        all_in(dense.at[hop, 1:SIDE], dense_rs.at[hop])
        for step in range(SIDE):
            held = u_own[:, HALVES[hop]] if step == 0 else dense[hop, step]
            top, low = halves(held)
            hot = hit[step * RUN : (step + 1) * RUN, :]
            rows = mm(hot, top, NN) + mm(hot, low, NN)
            for to in range(SIDE):
                part = rows[to * TOUCH : (to + 1) * TOUCH, :]
                if to:
                    relay_send[hop, to, step] = part
                elif hop == 0:
                    u_recv[0, 0, step, :, HALVES[0]] = part
                else:
                    u_recv[0, step, 0, :, HALVES[1]] = part
        for to in range(1, SIDE):
            relay_copy(hop, to).start()

    def select_rows(t):
        mask = mask_recv[:, t, :]
        before = onehot(iota((RUN, RUN), 0) < iota((RUN, RUN), 1))
        rank = mm(mask.astype(BF16), before, NN)
        spread = onehot(iota((OWNERS * TOUCH, OWNERS), 0) // TOUCH == iota((OWNERS * TOUCH, OWNERS), 1))
        rank_rows = mm(spread, rank.astype(BF16), NN)
        mask_rows = mm(spread, mask.astype(BF16), NN)
        index = (iota((OWNERS * TOUCH, RUN), 0) % TOUCH).astype(F32)
        hit = jnp.where(rank_rows == index, mask_rows, 0.0)
        if t:
            sel[...] = hit.astype(BF16)
        sel_t[t] = hit.T.astype(BF16)

    def send_rows():
        for group in range(GROUPS):
            hot = sel[rows_of(group), :]
            rows = mm(hot, u_parts[0], NN) + mm(hot, u_parts[1], NN)
            for slot in slots_of(group):
                part = rows[(slot % SIDE) * TOUCH : (slot % SIDE + 1) * TOUCH, :]
                if slot:
                    u_send[slot] = part
                else:
                    u_recv[1, 0, 0] = part
            for slot in slots_of(group):
                if slot:
                    u_copy(slot).start()

    def away_copy(group):
        return pltpu.make_async_remote_copy(
            src_ref=u_recv.at[subs - 1, group], dst_ref=away_rows.at[group],
            send_sem=away_ss, recv_sem=away_rs.at[group],
            device_id=(down, place), device_id_type=MESH)

    def away_items():
        t = subs - 1
        own = (own_hi[...], own_lo[...])
        for group in range(GROUPS):
            all_in(away_rows.at[group], away_rs.at[group])
            at = rows_of(group)
            top, low = halves(away_rows[group].reshape(RUN, -1))
            ut_hi[at, :] = top
            ut_lo[at, :] = low
            w_top, w_low = halves(rat[subs, at, :] - num[subs, at, :] * mm3((top, low), own, NT))
            w_hi[at, :] = w_top
            w_lo[at, :] = w_low
        for chunk in range(items // RUN):
            at = slice(chunk * RUN, (chunk + 1) * RUN)
            old = v_new[at, :]
            v_cur[at, :] = old + steps_of(t) * (item_grad(0, GROUPS, chunk) - 0.1 * old)

    def tile_rows(t):
        held = []
        for group in range(GROUPS):
            if group == GROUPS - 1 and t + 1 < subs:
                item_begin()
            rows_in(t, group)
            if t + 1 == subs:
                away_copy(group).start()
            if group == GROUPS - 1:
                for slot in held:
                    g_copy(t, slot).start()
            at = rows_of(group)
            top, low = halves(u_recv[t, group].reshape(RUN, -1))
            v = (v_hi[...], v_lo[...])
            w = rat[t, at, :] - num[t, at, :] * mm3((top, low), v, NT)
            w_top, w_low = halves(w)
            if t + 1 < subs:
                ut_hi[at, :] = top
                ut_lo[at, :] = low
                w_hi[at, :] = w_top
                w_lo[at, :] = w_low
            grad = mm3((w_top, w_low), v, NN)
            for slot in slots_of(group):
                part = grad[(slot % SIDE) * TOUCH : (slot % SIDE + 1) * TOUCH, :]
                if slot:
                    g_send[t, slot] = part
                else:
                    g_recv[t, slot] = part
            for slot in slots_of(group):
                if slot:
                    if False:
                        held.append(slot)
                    else:
                        g_copy(t, slot).start()

    def user_step(t):
        old = u_own[...]
        total = jnp.zeros_like(old)
        for group in range(GROUPS):
            grads_in(t, group)
            top, low = halves(g_recv[t, group * SIDE : (group + 1) * SIDE].reshape(RUN, -1))
            back = sel_t[t, :, rows_of(group)]
            total = total + mm(back, top, NN) + mm(back, low, NN)
        u_own[...] = old + steps_of(t) * (total - 0.1 * old)

    def update_half():
        all_in(dense.at[:, 1:SIDE], dense_ss)
        user_step(0)
        top, low = halves(u_own[...])
        u_parts[0] = top
        u_parts[1] = low
        send_rows()

    def v_copy(chunk):
        at = pl.ds(chunk * RUN, RUN)
        return pltpu.make_async_remote_copy(
            src_ref=v_new.at[at], dst_ref=v_in.at[at],
            send_sem=v_ss, recv_sem=v_rs,
            device_id=(up, place), device_id_type=MESH)

    def item_grad(first, last, chunk):
        at = slice(chunk * RUN, (chunk + 1) * RUN)
        rows = slice(first * RUN, last * RUN)
        return mm3((w_hi[rows, at], w_lo[rows, at]), (ut_hi[rows, :], ut_lo[rows, :]), TN)

    def item_begin():
        for chunk in range(items // RUN):
            v_new[chunk * RUN : (chunk + 1) * RUN, :] = item_grad(0, GROUPS - 1, chunk)

    def item_step_0():
        step = steps_of(0)
        for chunk in range(items // RUN):
            at = slice(chunk * RUN, (chunk + 1) * RUN)
            grad = v_new[at, :] + item_grad(GROUPS - 1, GROUPS, chunk)
            fresh = v_cur[at, :] + step * (grad - 0.1 * v_cur[at, :])
            v_new[at, :] = fresh
            v_copy(chunk).start()
            top, low = halves(fresh)
            own_hi[at, :] = top
            own_lo[at, :] = low

    load_u.wait()
    for step in range(1, SIDE):
        for hop in (1, 0):
            relay_mask_copy(hop, step).start()
    for step in (1, 3, 2):
        for hop in (1, 0):
            dense_copy(hop, step if hop == 0 else (0, 1, 3, 2)[step]).start()
    for slot in range(1, OWNERS):
        mask_copy(slot).start()
    pack_copy = pltpu.make_async_remote_copy(
        src_ref=pack_send, dst_ref=pack_recv, send_sem=pack_ss, recv_sem=pack_rs,
        device_id=(down, place), device_id_type=MESH)
    pack_copy.start()
    mask_recv[0] = mask_send[0, 0]

    load_v.wait()
    split_v()
    one_hot_items(0)
    counts_and_ratings(0)
    relay_out(1)
    relay_out(0)

    def wait_masks():
        all_in(mask_recv.at[1:OWNERS], mask_rs)

    tile_rows(0)
    item_step_0()
    wait_masks()
    select_rows(0)
    select_rows(1)
    one_hot_items(1)
    counts_and_ratings(1)
    update_half()

    def wait_v():
        all_in(v_in, v_rs)

    all_in(pack_recv, pack_rs)
    one_hot_items(2)
    counts_and_ratings(2)
    wait_v()
    top, low = halves(v_in[...])
    v_hi[...] = top
    v_lo[...] = low
    tile_rows(1)
    away_items()
    put_v = pltpu.make_async_copy(v_cur, out_v, load_sem.at[1])
    put_v.start()
    user_step(1)
    put_u = pltpu.make_async_copy(u_own, out_u, load_sem.at[0])
    put_u.start()

    def finish():
        all_in(mask_recv.at[1:OWNERS], mask_ss)
        all_in(relay_mask.at[:, 1:SIDE], relay_ms)
        all_in(u_send.at[1:OWNERS], u_ss)
        all_in(g_send.at[:, 1:OWNERS], g_ss)
        all_in(relay_send.at[:, 1:SIDE], relay_ss)
        all_in(pack_recv, pack_ss)
        all_in(away_rows, away_ss)
        all_in(v_in, v_ss)
        put_v.wait()
        put_u.wait()

    finish()


def on_device(n_rows, user_factors, item_factors, ratings, user_offsets, item_offsets, counts):
    users, rank = user_factors.shape
    items = item_factors.shape[0]
    subs, entries = ratings.shape
    picked = OWNERS * TOUCH
    vmem = pl.BlockSpec(memory_space=pltpu.VMEM)
    hbm = pl.BlockSpec(memory_space=pl.ANY)
    dma = pltpu.SemaphoreType.DMA
    return pl.pallas_call(
        functools.partial(kernel, n_rows),
        out_shape=(
            pltpu.VMEM((users, rank), F32),
            pltpu.VMEM((items, rank), F32),
        ),
        in_specs=[hbm, hbm, vmem, vmem, vmem, vmem],
        out_specs=(hbm, hbm),
        scratch_shapes=[
            pltpu.VMEM((users, rank), F32),
            pltpu.VMEM((items, rank), F32),
            pltpu.VMEM((items, rank), F32),
            pltpu.VMEM((items, rank), F32),
            pltpu.VMEM((items, rank), BF16),
            pltpu.VMEM((items, rank), BF16),
            pltpu.VMEM((GROUPS, SIDE, 8, RUN), F32),
            pltpu.VMEM((OWNERS, 8, RUN), F32),
            pltpu.VMEM((8, 128), F32),
            pltpu.VMEM((8, entries), F32),
            pltpu.VMEM((picked, RUN), BF16),
            pltpu.VMEM((subs, RUN, picked), BF16),
            pltpu.VMEM((items, entries), BF16),
            pltpu.VMEM((items, entries), BF16),
            pltpu.VMEM((items, entries), BF16),
            pltpu.VMEM((subs + 1, picked, items), F32),
            pltpu.VMEM((subs + 1, picked, items), F32),
            pltpu.VMEM((picked, rank), BF16),
            pltpu.VMEM((picked, rank), BF16),
            pltpu.VMEM((picked, items), BF16),
            pltpu.VMEM((picked, items), BF16),
            pltpu.VMEM((OWNERS, TOUCH, rank), F32),
            pltpu.VMEM((subs, GROUPS, SIDE, TOUCH, rank), F32),
            pltpu.VMEM((subs, OWNERS, TOUCH, rank), F32),
            pltpu.VMEM((subs, OWNERS, TOUCH, rank), F32),
            pltpu.VMEM((2, users, rank), BF16),
            pltpu.VMEM((2, SIDE, SIDE, 8, RUN), F32),
            pltpu.VMEM((2, SIDE, users, rank // 2), F32),
            pltpu.VMEM((2, SIDE, SIDE, TOUCH, rank // 2), F32),
            pltpu.VMEM((8, entries), F32),
            pltpu.VMEM((8, entries), F32),
            pltpu.VMEM((GROUPS, SIDE, TOUCH, rank), F32),
            pltpu.VMEM((items, rank), BF16),
            pltpu.VMEM((items, rank), BF16),
            dma,
            dma,
            dma,
            dma((GROUPS,)),
            dma,
            dma,
            dma,
            dma((2,)),
            dma((2,)),
            dma((2, SIDE)),
            dma((2,)),
            dma,
            dma,
            dma,
            dma((GROUPS,)),
            dma,
            dma((subs, GROUPS)),
            dma,
            dma,
        ],
        compiler_params=pltpu.CompilerParams(
            collective_id=0, has_side_effects=True, vmem_limit_bytes=56 * 1024 * 1024
        ),
        name="sgd",
    )(user_factors, item_factors, ratings, user_offsets, item_offsets, counts.T)


def solution(mesh):
    shard = P(("rows", "strata"), None)
    split = P(None, ("rows", "strata"))
    return jax.shard_map(
        functools.partial(on_device, mesh.shape["rows"]),
        mesh=mesh,
        in_specs=(shard, shard, split, split, split, split),
        out_specs=(shard, shard),
        check_vma=False,
    )
```

time: 76.8 us -> 73.1 us (0.952); the launches traced: 75.6 us -> 72.9 us
  Pallas kernels: 73.2 us -> 70.6 us
    pallas_call x1, Pallas kernels: 73.2 us -> 70.6 us  [on_device(): pl.pallas_call(functools.partial(kernel, n_rows), out_shape=(pltpu.VMEM((...]
where the time goes in v3:
time: 73.1 us; the launch traced here: 72.9 us
  Pallas kernels  70.6 us (97%)
  local copies, waits for them, and re-layouts  1.67 us (2%)
    pallas_call x1, Pallas kernels, on_device(): pl.pallas_call(functools.partial(kernel, n_rows), out_shape=(pltpu.VMEM((...  70.6 us
    unnamed x2, local copies, waits for them, and re-layouts  1.67 us

profile of v3, /device:TPU:96, one launch (start us, length us, event | category | flops | bytes accessed | tf_op | source)
XLA Modules:
  0.0 72.9 jit_solution(3376500410571327956)
XLA Ops:
  0.6 70.6 %sgd.1 = (f32[128,512]{1,0:T(8,128)S(1)}, f32[512,512]{1,0:T(8,128)S(1)}) custom-call(f32[128,512]{1,0:T(8,128)} %u_hbm.1, f32[512,512]{1,0:T(8,128)} %v_hbm.1, f32[2,1024]{1,0:T(2,128)} %rate_ref.1, s32[2,1024]{1,0:T(2,128)} %user_ref.1, s32[2,1024]{1,0:T(2,128)} %item_ref.1, s32[1,2]{1,0:T(1,128)} %bitcast.1), custom_call_target="tpu_custom_call" | custom-call | tf_op jit(solution)/shard_map/sgd/pallas_call | solution.py:471
  71.2 0.7 copy.10
  71.9 1.0 %copy.11 = f32[512,512]{1,0:T(8,128)} copy(f32[512,512]{1,0:T(8,128)S(1)} %get-tuple-element.3) | data formatting | bytes 2097152

commit v4 on v3

--- a/solution.py
+++ b/solution.py
@@ -313,16 +313,10 @@
             v_cur[at, :] = old + steps_of(t) * (item_grad(0, GROUPS, chunk) - 0.1 * old)
 
     def tile_rows(t):
-        held = []
         for group in range(GROUPS):
-            if group == GROUPS - 1 and t + 1 < subs:
-                item_begin()
             rows_in(t, group)
             if t + 1 == subs:
                 away_copy(group).start()
-            if group == GROUPS - 1:
-                for slot in held:
-                    g_copy(t, slot).start()
             at = rows_of(group)
             top, low = halves(u_recv[t, group].reshape(RUN, -1))
             v = (v_hi[...], v_lo[...])
@@ -342,10 +336,7 @@
                     g_recv[t, slot] = part
             for slot in slots_of(group):
                 if slot:
-                    if False:
-                        held.append(slot)
-                    else:
-                        g_copy(t, slot).start()
+                    g_copy(t, slot).start()
 
     def user_step(t):
         old = u_own[...]
@@ -377,15 +368,11 @@
         rows = slice(first * RUN, last * RUN)
         return mm3((w_hi[rows, at], w_lo[rows, at]), (ut_hi[rows, :], ut_lo[rows, :]), TN)
 
-    def item_begin():
-        for chunk in range(items // RUN):
-            v_new[chunk * RUN : (chunk + 1) * RUN, :] = item_grad(0, GROUPS - 1, chunk)
-
     def item_step_0():
         step = steps_of(0)
         for chunk in range(items // RUN):
             at = slice(chunk * RUN, (chunk + 1) * RUN)
-            grad = v_new[at, :] + item_grad(GROUPS - 1, GROUPS, chunk)
+            grad = item_grad(0, GROUPS, chunk)
             fresh = v_cur[at, :] + step * (grad - 0.1 * v_cur[at, :])
             v_new[at, :] = fresh
             v_copy(chunk).start()
@@ -400,6 +387,12 @@
     for step in (1, 3, 2):
         for hop in (1, 0):
             dense_copy(hop, step if hop == 0 else (0, 1, 3, 2)[step]).start()
+    load_v.wait()
+    split_v()
+    one_hot_items(0)
+    counts_and_ratings(0)
+    relay_out(1)
+    relay_out(0)
     for slot in range(1, OWNERS):
         mask_copy(slot).start()
     pack_copy = pltpu.make_async_remote_copy(
@@ -408,12 +401,6 @@
     pack_copy.start()
     mask_recv[0] = mask_send[0, 0]
 
-    load_v.wait()
-    split_v()
-    one_hot_items(0)
-    counts_and_ratings(0)
-    relay_out(1)
-    relay_out(0)
 
     def wait_masks():
         all_in(mask_recv.at[1:OWNERS], mask_rs)

time: 73.1 us -> 72.2 us (0.988)
  Pallas kernels: 70.6 us -> 69.4 us
    pallas_call x1, Pallas kernels: 70.6 us -> 69.4 us  [on_device(): pl.pallas_call(functools.partial(kernel, n_rows), out_shape=(pltpu.VMEM((...]
where the time goes in v4:
time: 72.2 us; the launch traced here: 71.7 us
  Pallas kernels  69.4 us (96%)
  local copies, waits for them, and re-layouts  1.67 us (2%)
    pallas_call x1, Pallas kernels, on_device(): pl.pallas_call(functools.partial(kernel, n_rows), out_shape=(pltpu.VMEM((...  69.4 us
    unnamed x2, local copies, waits for them, and re-layouts  1.67 us

profile of v4, /device:TPU:96, one launch (start us, length us, event | category | flops | bytes accessed | tf_op | source)
XLA Modules:
  0.0 71.7 jit_solution(6640880199200525898)
XLA Ops:
  0.6 69.4 %sgd.1 = (f32[128,512]{1,0:T(8,128)S(1)}, f32[512,512]{1,0:T(8,128)S(1)}) custom-call(f32[128,512]{1,0:T(8,128)} %u_hbm.1, f32[512,512]{1,0:T(8,128)} %v_hbm.1, f32[2,1024]{1,0:T(2,128)} %rate_ref.1, s32[2,1024]{1,0:T(2,128)} %user_ref.1, s32[2,1024]{1,0:T(2,128)} %item_ref.1, s32[1,2]{1,0:T(1,128)} %bitcast.1), custom_call_target="tpu_custom_call" | custom-call | tf_op jit(solution)/shard_map/sgd/pallas_call | solution.py:458
  70.0 0.7 copy.10
  70.8 1.0 %copy.11 = f32[512,512]{1,0:T(8,128)} copy(f32[512,512]{1,0:T(8,128)S(1)} %get-tuple-element.3) | data formatting | bytes 2097152

commit v5 on v4

--- a/solution.py
+++ b/solution.py
@@ -155,7 +155,7 @@
         all_in(g_recv.at[t, first : (group + 1) * SIDE], g_rs.at[t, group])
 
     def slots_of(group):
-        return range(group * SIDE, (group + 1) * SIDE)
+        return [group * SIDE + step for step in STEPS]
 
     def rows_of(group):
         return slice(group * RUN, (group + 1) * RUN)

time: 72.2 us -> 70.8 us (0.981)
  Pallas kernels: 69.4 us -> 68.3 us
    pallas_call x1, Pallas kernels: 69.4 us -> 68.3 us  [on_device(): pl.pallas_call(functools.partial(kernel, n_rows), out_shape=(pltpu.VMEM((...]
where the time goes in v5:
time: 70.8 us; the launch traced here: 70.7 us
  Pallas kernels  68.3 us (96%)
  local copies, waits for them, and re-layouts  1.67 us (2%)
    pallas_call x1, Pallas kernels, on_device(): pl.pallas_call(functools.partial(kernel, n_rows), out_shape=(pltpu.VMEM((...  68.3 us
    unnamed x2, local copies, waits for them, and re-layouts  1.67 us

profile of v5, /device:TPU:96, one launch (start us, length us, event | category | flops | bytes accessed | tf_op | source)
XLA Modules:
  0.0 70.7 jit_solution(15841608293691809363)
XLA Ops:
  0.6 68.3 %sgd.1 = (f32[128,512]{1,0:T(8,128)S(1)}, f32[512,512]{1,0:T(8,128)S(1)}) custom-call(f32[128,512]{1,0:T(8,128)} %u_hbm.1, f32[512,512]{1,0:T(8,128)} %v_hbm.1, f32[2,1024]{1,0:T(2,128)} %rate_ref.1, s32[2,1024]{1,0:T(2,128)} %user_ref.1, s32[2,1024]{1,0:T(2,128)} %item_ref.1, s32[1,2]{1,0:T(1,128)} %bitcast.1), custom_call_target="tpu_custom_call" | custom-call | tf_op jit(solution)/shard_map/sgd/pallas_call | solution.py:458
  69.0 0.7 copy.10
  69.7 1.0 %copy.11 = f32[512,512]{1,0:T(8,128)} copy(f32[512,512]{1,0:T(8,128)S(1)} %get-tuple-element.3) | data formatting | bytes 2097152
